TPU v7x, 128 devices: a whole 4x4x4 slice. The times are simulated.
128 devices in a mesh: wide: 32 (over y, x, core), narrow: 4 (over z).
Axes of the slice: x: 4, y: 4, z: 4, core: 2. Of those that a mesh axis runs over, the one named last changes fastest.
Arguments:
- slab: float32 [96, 512, 8192], P('narrow', 'wide'), may hold values from -24 to 24, as said below
- start: float32 [512, 64], replicated, may hold values from -6 to 6
Outputs:
- core: float32 [96, 64, 8192], P('narrow', None, 'wide')
- factor: float32 [512, 64], replicated
Inputs may be any that keep to these rules, and one draw needn't show every extreme that they name: The slab is a planted sum of 64 separable terms plus noise.
All inputs are finite; a program needn't handle non-finite values.
Results may differ from a plain program's by a relative error of at most 0.0003.
Values sent between devices are 32-bit elements; how exact they have to be, the bound alone decides.
A program may use at most 256 MiB of HBM per device.

v0:
```python
import jax
import jax.numpy as jnp
from jax import lax
from jax.sharding import PartitionSpec as P

ITERS = 2


def orthonormal(matrix):
    product = jnp.dot(matrix.T, matrix, precision=lax.Precision.HIGHEST)
    lower = jnp.linalg.cholesky(product)
    return lax.linalg.triangular_solve(lower, matrix, left_side=False, lower=True, transpose_a=True)


def block_gram(block):
    return jnp.einsum("nix,njx->ij", block, block, precision=lax.Precision.HIGHEST)


def on_device(slab, start):
    fibres = lax.all_to_all(slab, "wide", split_axis=2, concat_axis=1, tiled=True)
    local_gram = block_gram(fibres)
    basis = orthonormal(start)
    gram = lax.psum(local_gram, ("wide", "narrow"))
    for step in range(ITERS):
        basis = orthonormal(jnp.dot(gram, basis, precision=lax.Precision.HIGHEST))
    core = jnp.einsum("ik,sif->skf", basis, fibres, precision=lax.Precision.HIGHEST)
    return (core, basis)


def solution(mesh):
    placed = (P("narrow", "wide", None), P())
    return jax.shard_map(
        on_device,
        mesh=mesh,
        in_specs=placed,
        out_specs=(P("narrow", None, "wide"), P()),
        check_vma=False,
    )
```

profile of v0, /device:TPU:1, one launch (start us, length us, event | category | flops | bytes accessed | tf_op | source)
XLA Modules:
  0.0 642.3 jit_solution(10626874872593620060)
XLA Ops:
  7.2 33.5 %copy.13 = f32[24,16,8192]{0,1,2:T(8,128)} copy(f32[24,16,8192]{2,1,0:T(8,128)} %param.5) | data formatting | bytes 25165824 | tf_op args[0]
  40.7 57.8 %reshape.27 = f32[32,1,98304]{2,1,0:T(1,128)} reshape(f32[8192,16,24]{2,1,0:T(8,128)} %bitcast.44) | data formatting | bytes 25165824
  98.5 8.6 %all-to-all-start = ((f32[32,1,98304]{2,1,0:T(1,128)}), f32[32,1,98304]{2,1,0:T(1,128)}, u32[]{:S(2)}, u32[]{:S(2)}) async-start(f32[32,1,98304]{2,1,0:T(1,128)} %reshape.27), calls=%async_computation | async-start | bytes 25165824 | tf_op jit(solution)/shard_map/all_to_all | solution.py:20
  107.2 0.3 fusion.15
  107.5 0.1 copy.15
  107.6 5.8 cholesky.59
  113.5 145.2 %all-to-all-done = f32[32,1,98304]{2,1,0:T(1,128)} async-done(((f32[32,1,98304]{2,1,0:T(1,128)}), f32[32,1,98304]{2,1,0:T(1,128)}, u32[]{:S(2)}, u32[]{:S(2)}) %all-to-all-start) | async-done | bytes 12582944 | tf_op jit(solution)/shard_map/all_to_all | solution.py:20
  258.7 0.5 broadcast.37
  259.2 36.7 %reduce.4 = f32[32,98304]{1,0:T(8,128)} reduce(f32[32,1,98304]{2,1,0:T(1,128)} %all-to-all-done, f32[]{:T(128)} %broadcast.37), dimensions={1}, to_apply=%all_to_all.13.reduce_sub_computation | reduce | bytes 25165828 | tf_op jit(solution)/shard_map/all_to_all | solution.py:20
  296.0 78.6 %reshape.28 = f32[8192,16,24]{2,1,0:T(8,128)} reshape(f32[32,98304]{1,0:T(8,128)} %reduce.4) | data formatting | bytes 25165824
  374.6 40.1 %copy.14 = f32[24,16,32,256]{3,1,2,0:T(8,128)} copy(f32[24,16,32,256]{0,1,3,2:T(8,128)} %bitcast) | data formatting | bytes 25165824 | tf_op jit(solution)/shard_map/all_to_all | solution.py:20
  414.7 24.7 %convolution_bitcast_fusion.1 = f32[512,512]{1,0:T(8,128)} fusion(f32[24,512,256]{2,1,0:T(8,128)} %bitcast.62), kind=kOutput, calls=%fused_computation.1 | convolution fusion | flops 19327352832 | bytes 13631488 | tf_op jit(solution)/shard_map/nix,njx->ij/dot_general | solution.py:16
  439.5 0.6 compare_reduce_fusion.2
  440.1 0.7 fusion.1
  440.8 4.9 custom-call.7
  445.7 0.3 convolution_bitcast_fusion.3
  446.0 147.3 %all-reduce.2.cloned.1.call-done = f32[512,512]{1,0:T(8,128)} async-done(((f32[512,512]{1,0:T(8,128)}), f32[512,512]{1,0:T(8,128)}) %all-reduce.2.cloned.1.call-update) | async-done | bytes 1048592 | tf_op jit(solution)/shard_map/psum | solution.py:23
  593.3 2.4 fusion.16
  595.7 0.3 fusion.17
  596.1 5.8 cholesky.70
  601.9 0.6 compare_reduce_fusion.1
  602.6 0.7 fusion.2
  603.3 4.9 custom-call.8
  608.1 0.3 convolution_bitcast_fusion.2
  608.5 2.4 fusion.18
  610.8 0.3 fusion.19
  611.2 5.8 cholesky.81
  617.1 0.6 compare_reduce_fusion
  617.7 0.7 fusion.3
  618.4 4.9 custom-call.9
  623.3 0.3 fusion.4
  623.6 11.8 %convolution_bitcast_fusion = f32[24,64,256]{2,1,0:T(8,128)} fusion(f32[24,512,256]{2,1,0:T(8,128)} %bitcast.63, f32[64,512]{1,0:T(8,128)S(1)} %fusion.4), kind=kOutput, calls=%fused_computation | convolution fusion | flops 2415919104 | bytes 14286848 | tf_op jit(solution)/shard_map/ik,sif->skf/dot_general | solution.py:26
  (14 shorter events, 0.3 us)
Async XLA Ops:
  7.2 100.1 %copy-start = (f32[512,64]{0,1:T(8,128)S(1)}, f32[512,64]{0,1:T(8,128)}, u32[]{:S(2)}) copy-start(f32[512,64]{0,1:T(8,128)} %param.6) | copy-start | bytes 393220
  98.5 160.2 %all-to-all-start = ((f32[32,1,98304]{2,1,0:T(1,128)}), f32[32,1,98304]{2,1,0:T(1,128)}, u32[]{:S(2)}, u32[]{:S(2)}) async-start(f32[32,1,98304]{2,1,0:T(1,128)} %reshape.27), calls=%async_computation | async-start | bytes 25165824 | tf_op jit(solution)/shard_map/all_to_all | solution.py:20
  107.2 486.2 %all-reduce.2.cloned.1.call-start = ((), (), s32[]{:S(2)}) async-start(), calls=%async_computation.1 | async-start | bytes 2097152 | tf_op jit(solution)/shard_map/psum | solution.py:23
  623.6 11.8 %copy-start.1 = (f32[64,512]{1,0:T(8,128)}, f32[64,512]{1,0:T(8,128)S(1)}, u32[]{:S(2)}) copy-start(f32[64,512]{1,0:T(8,128)S(1)} %fusion.4) | copy-start | bytes 393220
Sparse Core Ops, SparseCore 0:
  439.6 153.6 all-reduce.1
where the time goes:
time: 645 us; the launch traced here: 642 us
  waiting for transfers between devices  293 us (45%)
  local copies, waits for them, and re-layouts  211 us (33%)
  other arithmetic  73 us (11%)
  matrix products  43 us (7%)
  between operations  14.2 us (2%)
  starting transfers between devices  8.68 us (1%)
    unnamed x7, local copies, waits for them, and re-layouts  170 us
    psum x1, waiting for transfers between devices, on_device(): gram = lax.psum(local_gram, ('wide', 'narrow'))  147 us
    all_to_all x1, waiting for transfers between devices, on_device(): lax.all_to_all(slab, 'wide', split_axis=2, concat_axis=1, tiled=True)  145 us
    all_to_all x2, local copies, waits for them, and re-layouts, on_device(): lax.all_to_all(slab, 'wide', split_axis=2, concat_axis=1, tiled=True)  40.6 us
    all_to_all x1, other arithmetic, on_device(): lax.all_to_all(slab, 'wide', split_axis=2, concat_axis=1, tiled=True)  36.7 us
    dot_general x1, matrix products, block_gram(): jnp.einsum('nix,njx->ij', block, block, precision=lax.Precision.HIGHEST)  24.7 us
    another operation x9, other arithmetic, orthonormal(): lower = jnp.linalg.cholesky(product)  19.6 us
    another operation x6, other arithmetic, orthonormal(): lax.linalg.triangular_solve(lower, matrix, left_side=False, lower=True, t...  16.6 us
  transfers between devices with their start and end apart: 2, of which 2 were waited for; matrix products, arithmetic and copies ran while one was open for 2% of the time, Pallas kernels for 0%

commit v1 on v0

--- a/solution.py
+++ b/solution.py
@@ -17,7 +17,12 @@
 
 
 def on_device(slab, start):
-    fibres = lax.all_to_all(slab, "wide", split_axis=2, concat_axis=1, tiled=True)
+    fibres = jnp.concatenate(
+        jax.lax.all_to_all(
+            jnp.stack(jnp.split(slab, jax.lax.axis_size("wide"), 2), axis=0), "wide", 0, 0
+        ),
+        axis=1,
+    )
     local_gram = block_gram(fibres)
     basis = orthonormal(start)
     gram = lax.psum(local_gram, ("wide", "narrow"))

time: 645 us -> 465 us (0.72)
  local copies, waits for them, and re-layouts: 211 us -> 68.5 us
  other arithmetic: 73 us -> 36.2 us
    unnamed x7 -> x35, local copies, waits for them, and re-layouts: 170 us -> 55.1 us
    all_to_all x2 -> x0, local copies, waits for them, and re-layouts: 40.6 us -> none  [on_device(): lax.all_to_all(slab, 'wide', split_axis=2, concat_axis=1, tiled=True)]
    all_to_all x1 -> x0, other arithmetic: 36.7 us -> none  [on_device(): lax.all_to_all(slab, 'wide', split_axis=2, concat_axis=1, tiled=True)]
    reshape x0 -> x1, local copies, waits for them, and re-layouts: none -> 11.4 us  [on_device(): jnp.concatenate(jax.lax.all_to_all(jnp.stack(jnp.split(slab, jax.lax.axis...]
  transfers between devices with their start and end apart: 2 -> 2, of which waited for: 2 -> 2; matrix products, arithmetic and copies ran while one was open for 2% -> 3% of each run, Pallas kernels for 0% -> 0%
where the time goes in v1:
time: 465 us; the launch traced here: 464 us
  waiting for transfers between devices  293 us (63%)
  local copies, waits for them, and re-layouts  68.5 us (15%)
  matrix products  43.6 us (9%)
  other arithmetic  36.2 us (8%)
  between operations  14.2 us (3%)
  starting transfers between devices  8.68 us (2%)
    psum x1, waiting for transfers between devices, on_device(): gram = lax.psum(local_gram, ('wide', 'narrow'))  147 us
    all_to_all x1, waiting for transfers between devices, on_device(): jax.lax.all_to_all(jnp.stack(jnp.split(slab, jax.lax.axis_size('wide'), 2...  145 us
    unnamed x35, local copies, waits for them, and re-layouts  55.1 us
    dot_general x1, matrix products, block_gram(): jnp.einsum('nix,njx->ij', block, block, precision=lax.Precision.HIGHEST)  24.7 us
    another operation x9, other arithmetic, orthonormal(): lower = jnp.linalg.cholesky(product)  19.6 us
    another operation x6, other arithmetic, orthonormal(): lax.linalg.triangular_solve(lower, matrix, left_side=False, lower=True, t...  16.6 us
    dot_general x1, matrix products, on_device(): jnp.einsum('ik,sif->skf', basis, fibres, precision=lax.Precision.HIGHEST)  12.4 us
    reshape x1, local copies, waits for them, and re-layouts, on_device(): jnp.concatenate(jax.lax.all_to_all(jnp.stack(jnp.split(slab, jax.lax.axis...  11.4 us
  transfers between devices with their start and end apart: 2, of which 2 were waited for; matrix products, arithmetic and copies ran while one was open for 3% of the time, Pallas kernels for 0%

profile of v1, /device:TPU:1, one launch (start us, length us, event | category | flops | bytes accessed | tf_op | source)
XLA Modules:
  0.0 463.8 jit_solution(6301869120156648215)
XLA Ops:
  7.2 1.8 bitcast_dynamic-update-slice_fusion.31
  12.5 1.8 bitcast_dynamic-update-slice_fusion.28
  16.1 1.8 bitcast_dynamic-update-slice_fusion.26
  19.6 1.8 bitcast_dynamic-update-slice_fusion.24
  28.4 1.8 bitcast_dynamic-update-slice_fusion.19
  30.2 1.8 bitcast_dynamic-update-slice_fusion.18
  32.0 1.8 bitcast_dynamic-update-slice_fusion.17
  33.8 1.8 bitcast_dynamic-update-slice_fusion.16
  35.6 1.8 bitcast_dynamic-update-slice_fusion.15
  37.4 1.8 bitcast_dynamic-update-slice_fusion.14
  39.1 1.8 bitcast_dynamic-update-slice_fusion.13
  44.4 1.8 bitcast_dynamic-update-slice_fusion.10
  46.3 1.8 bitcast_dynamic-update-slice_fusion.9
  48.0 1.8 bitcast_dynamic-update-slice_fusion.8
  51.6 1.8 bitcast_dynamic-update-slice_fusion.6
  55.2 1.8 bitcast_dynamic-update-slice_fusion.4
  57.0 1.8 bitcast_dynamic-update-slice_fusion.3
  62.3 1.8 bitcast_dynamic-update-slice_fusion
  64.0 8.6 %all-to-all-start = ((f32[32,24,16,256]{3,2,1,0:T(8,128)}), f32[32,24,16,256]{3,2,1,0:T(8,128)}, u32[]{:S(2)}, u32[]{:S(2)}) async-start(f32[32,24,16,256]{3,2,1,0:T(8,128)} %bitcast_dynamic-update-slice_fusion), calls=%async_computation | async-start | bytes 25165824 | tf_op jit(solution)/shard_map/all_to_all | solution.py:21
  73.1 5.8 %cholesky.59 = f32[64,64]{1,0:T(8,128)S(1)} custom-call(f32[64,64]{1,0:T(8,128)S(1)} %fusion.10), custom_call_target="Cholesky" | custom-call | tf_op jit(solution)/shard_map/jit(cholesky)/cholesky | solution.py:11
  79.0 145.2 %all-to-all-done = f32[32,24,16,256]{3,2,1,0:T(8,128)} async-done(((f32[32,24,16,256]{3,2,1,0:T(8,128)}), f32[32,24,16,256]{3,2,1,0:T(8,128)}, u32[]{:S(2)}, u32[]{:S(2)}) %all-to-all-start) | async-done | bytes 12582944 | tf_op jit(solution)/shard_map/all_to_all | solution.py:21
  224.2 11.4 %copy.4 = f32[24,32,16,256]{3,2,1,0:T(8,128)} copy(f32[24,32,16,256]{3,2,0,1:T(8,128)} %bitcast.32) | data formatting | bytes 25165824 | tf_op jit(solution)/shard_map/reshape | solution.py:20
  235.6 24.7 %convolution_bitcast_fusion.1 = f32[512,512]{1,0:T(8,128)} fusion(f32[24,512,256]{2,1,0:T(8,128)} %bitcast.122), kind=kOutput, calls=%fused_computation.1 | convolution fusion | flops 19327352832 | bytes 13631488 | tf_op jit(solution)/shard_map/nix,njx->ij/dot_general | solution.py:16
  261.7 4.9 %custom-call.7 = f32[1,64,64]{1,2,0:T(8,128)S(1)} custom-call(f32[1,64,64]{2,1,0:T(8,128)S(1)} %fusion.1), custom_call_target="InvertDiagBlocksLowerTriangular" | custom-call | tf_op jit(solution)/shard_map/triangular_solve/custom-call.0 | solution.py:12
  266.9 147.3 %all-reduce.2.cloned.1.call-done = f32[512,512]{1,0:T(8,128)} async-done(((f32[512,512]{1,0:T(8,128)}), f32[512,512]{1,0:T(8,128)}) %all-reduce.2.cloned.1.call-update) | async-done | bytes 1048592 | tf_op jit(solution)/shard_map/psum | solution.py:28
  414.2 2.4 fusion.16
  417.0 5.8 %cholesky.70 = f32[64,64]{1,0:T(8,128)S(1)} custom-call(f32[64,64]{1,0:T(8,128)S(1)} %fusion.8), custom_call_target="Cholesky" | custom-call | tf_op jit(solution)/shard_map/jit(cholesky)/cholesky | solution.py:11
  424.1 4.9 %custom-call.8 = f32[1,64,64]{1,2,0:T(8,128)S(1)} custom-call(f32[1,64,64]{2,1,0:T(8,128)S(1)} %fusion.2), custom_call_target="InvertDiagBlocksLowerTriangular" | custom-call | tf_op jit(solution)/shard_map/triangular_solve/custom-call.0 | solution.py:12
  429.4 2.4 fusion.18
  432.1 5.8 %cholesky.81 = f32[64,64]{1,0:T(8,128)S(1)} custom-call(f32[64,64]{1,0:T(8,128)S(1)} %fusion.6), custom_call_target="Cholesky" | custom-call | tf_op jit(solution)/shard_map/jit(cholesky)/cholesky | solution.py:11
  439.3 4.9 %custom-call.9 = f32[1,64,64]{1,2,0:T(8,128)S(1)} custom-call(f32[1,64,64]{2,1,0:T(8,128)S(1)} %fusion.3), custom_call_target="InvertDiagBlocksLowerTriangular" | custom-call | tf_op jit(solution)/shard_map/triangular_solve/custom-call.0 | solution.py:12
  444.5 12.4 %convolution_bitcast_fusion = f32[24,64,256]{2,1,0:T(8,128)} fusion(f32[24,512,256]{2,1,0:T(8,128)} %bitcast.123, f32[64,512]{1,0:T(8,128)S(1)} %fusion.4), kind=kOutput, calls=%fused_computation | convolution fusion | flops 2415919104 | bytes 14286848 | tf_op jit(solution)/shard_map/ik,sif->skf/dot_general | solution.py:31
  (41 shorter events, 30.8 us)
Async XLA Ops:
  7.2 65.6 %copy-start = (f32[512,64]{0,1:T(8,128)S(1)}, f32[512,64]{0,1:T(8,128)}, u32[]{:S(2)}) copy-start(f32[512,64]{0,1:T(8,128)} %param.6) | copy-start | bytes 393220
  64.0 160.2 %all-to-all-start = ((f32[32,24,16,256]{3,2,1,0:T(8,128)}), f32[32,24,16,256]{3,2,1,0:T(8,128)}, u32[]{:S(2)}, u32[]{:S(2)}) async-start(f32[32,24,16,256]{3,2,1,0:T(8,128)} %bitcast_dynamic-update-slice_fusion), calls=%async_computation | async-start | bytes 25165824 | tf_op jit(solution)/shard_map/all_to_all | solution.py:21
  72.7 341.5 %all-reduce.2.cloned.1.call-start = ((), (), s32[]{:S(2)}) async-start(), calls=%async_computation.1 | async-start | bytes 2097152 | tf_op jit(solution)/shard_map/psum | solution.py:28
  444.5 12.4 %copy-start.1 = (f32[64,512]{1,0:T(8,128)}, f32[64,512]{1,0:T(8,128)S(1)}, u32[]{:S(2)}) copy-start(f32[64,512]{1,0:T(8,128)S(1)} %fusion.4) | copy-start | bytes 393220
Sparse Core Ops, SparseCore 0:
  260.5 153.6 all-reduce.1
